TPU v7x, 256 devices: a whole 4x4x8 slice. The times are simulated.
256 devices in a mesh: region: 32 (over x, z), comm: 8 (over y, core).
Axes of the slice: x: 4, y: 4, z: 8, core: 2. Of those that a mesh axis runs over, the one named last changes fastest.
Arguments:
- cost: float32 [128, 262144], P('comm', 'region'), may hold values from 0.01 to 15, as said below
- flow_start: float32 [128, 262144], P('comm', 'region'), may hold values from 0 to 0.5
- capacity: float32 [262144], P('region'), may hold values from 5 to 135, as said below
- cap_dual_start: float32 [262144], P('region'), may hold values from 0 to 1
- demand: float32 [128, 131072], P('comm', 'region'), may hold values from -24 to 24
- node_dual_start: float32 [128, 131072], P('comm', 'region'), may hold values from -6 to 6
- incidence: float32 [4096, 128, 128], P('region'), may hold values from -0.25 to 0.25
- block_node: int32 [4096], P('region'), may hold values from 0 to 39
- ghost_source: int32 [256], P('region'), may hold values from 0 to 127, as said below
Outputs:
- final_flow: float32 [128, 262144], P('comm', 'region')
- final_cap_dual: float32 [262144], P('region')
- final_node_dual: float32 [128, 131072], P('comm', 'region')
Inputs may be any that keep to these rules, and one draw needn't show every extreme that they name: Each cost is positive. Each capacity is positive. `ghost_source`: ghost slot g of region r names boundary block j of region q as q * 4 + j. Slot 0 of every region has q = r + 16 in cyclic order; every other slot has q at most two regions from r in cyclic order (q may be r).
All inputs are finite; a program needn't handle non-finite values.
Results may differ from a plain program's by a relative error of at most 0.00021.
Values sent between devices are 32-bit elements; how exact they have to be, the bound alone decides.
A program may use at most 64 MiB of HBM per device.

v0:
```python
import jax
import jax.numpy as jnp
from jax import lax
from jax.sharding import PartitionSpec as P

BPA = 2
NBD = 4
NG = 8
ITERS = 2
step_scale = 0.08
highest = lax.Precision.HIGHEST


def pick_blocks(bnd_table, indices, commodities, count, block_width):
    return jnp.take(bnd_table.reshape(commodities, count, block_width), indices, axis=1)


def body(
    cost,
    flow_start,
    capacity,
    cap_dual_start,
    demand,
    node_dual_start,
    incidence,
    block_node,
    ghost_source,
):
    commodities, arc_count = cost.shape
    block_count, block_width, _ = incidence.shape
    own_blocks = demand.shape[1] // block_width
    region_total = lax.axis_size("region")
    bound_all = region_total * NBD
    slot_count = own_blocks + NG
    cost_sq = jnp.sum(cost * cost)
    demand_sq = jnp.sum(demand * demand)
    capacity_sq = jnp.sum(capacity * capacity)
    cost_all, demand_all = lax.psum((cost_sq, demand_sq), ("region", "comm"))
    capacity_all = lax.psum(capacity_sq, "region")
    weight = jnp.sqrt(cost_all / (demand_all + capacity_all))
    primal_step = step_scale / weight
    dual_step = step_scale * weight
    slot_table = (block_node[:, None] == jnp.arange(slot_count, dtype=jnp.int32)[None, :]).astype(
        jnp.float32
    )
    ghost_table = (ghost_source[:, None] == jnp.arange(bound_all, dtype=jnp.int32)[None, :]).astype(
        jnp.float32
    )
    flow_now, cap_dual, node_dual = (flow_start, cap_dual_start, node_dual_start)
    edge_cols = NBD * block_width
    for iteration in range(ITERS):
        bnd_table = lax.all_gather(node_dual[:, :edge_cols], "region", axis=1, tiled=True)
        ghost_duals = pick_blocks(bnd_table, ghost_source, commodities, bound_all, block_width)
        dual_blocks = jnp.concatenate(
            [node_dual.reshape(commodities, own_blocks, block_width), ghost_duals], axis=1
        )
        chosen_duals = jnp.take(dual_blocks, block_node, axis=1)
        back_term = jnp.einsum("kbn,bna->kba", chosen_duals, incidence, precision=highest)
        back_term = (
            back_term.reshape(commodities, block_count // BPA, BPA, block_width)
            .sum(axis=2)
            .reshape(commodities, arc_count)
        )
        flow_new = jnp.maximum(flow_now - primal_step * (cost - back_term + cap_dual[None, :]), 0.0)
        flow_bar = 2.0 * flow_new - flow_now
        arc_load = jnp.sum(flow_bar, axis=0)
        load_total = lax.psum(arc_load, "comm")
        cap_dual = jnp.maximum(cap_dual + dual_step * (load_total - capacity), 0.0)
        repeated_flow = jnp.repeat(
            flow_bar.reshape(commodities, arc_count // block_width, block_width), BPA, axis=1
        )
        forward = jnp.einsum("kba,bna->kbn", repeated_flow, incidence, precision=highest)
        slot_rows = jnp.einsum("kbn,bs->ksn", forward, slot_table, precision=highest)
        own_rows = slot_rows[:, :own_blocks]
        routed = jnp.einsum(
            "kgn,gb->kbn", slot_rows[:, own_blocks:], ghost_table, precision=highest
        )
        arrived = lax.psum_scatter(routed, "region", scatter_dimension=1, tiled=True)
        node_rows = jnp.concatenate([own_rows[:, :NBD] + arrived, own_rows[:, NBD:]], axis=1)
        node_dual = node_dual + dual_step * (
            demand - node_rows.reshape(commodities, own_blocks * block_width)
        )
        flow_now = flow_new
    return (flow_now, cap_dual, node_dual)


def solution(mesh):
    return jax.shard_map(
        body,
        mesh=mesh,
        in_specs=(
            P("comm", "region"),
            P("comm", "region"),
            P("region"),
            P("region"),
            P("comm", "region"),
            P("comm", "region"),
            P("region", None, None),
            P("region"),
            P("region"),
        ),
        out_specs=(P("comm", "region"), P("region"), P("comm", "region")),
        check_vma=False,
    )
```

profile of v0, /device:TPU:8, one launch (start us, length us, event | category | flops | bytes accessed | tf_op | source)
XLA Modules:
  0.0 738.6 jit_solution(913210635620972559)
XLA Ops:
  7.2 1.5 slice.30
  8.7 0.0 reduce-scatter.3.cloned.1.call-start
  8.8 1.6 multiply_reduce_fusion.1
  10.4 1.8 multiply_reduce_fusion
  12.2 1.4 multiply_reduce_fusion.2
  13.6 79.2 %all-reduce = (f32[]{:T(128)}, f32[]{:T(128)}) all-reduce(f32[]{:T(128)} %multiply_reduce_fusion, f32[]{:T(128)} %multiply_reduce_fusion.1), channel_id=1, replica_groups=mesh['region'=32,'comm'=8] {'region','comm'}, use_global_device_ids=true, to_apply=%region_1.0 | all-reduce | flops 2 | bytes 16 | tf_op jit(solution)/shard_map/psum | solution.py:38
  92.9 73.2 %psum.37 = f32[]{:T(128)} all-reduce(f32[]{:T(128)} %multiply_reduce_fusion.2), channel_id=1, replica_groups=mesh['region'=32,'comm'=8] {'region'}, use_global_device_ids=true, to_apply=%region_5.0 | all-reduce | flops 1 | bytes 8 | tf_op jit(solution)/shard_map/psum | solution.py:39
  168.2 0.7 compare_select_fusion.1
  168.8 0.7 compare_select_fusion
  169.5 0.7 compare_and_fusion
  170.1 0.7 compare_and_fusion.1
  170.8 1.0 copy_bitcast_fusion.5
  171.8 1.3 copy_bitcast_fusion.1
  173.1 0.6 gather_fusion
  173.7 0.1 select_bitcast_fusion.1
  173.8 0.8 gather_fusion.1
  174.6 9.6 %bitcast_reduce_fusion.1 = f32[16,64,128]{2,0,1:T(8,128)S(1)} fusion(f32[128,128,128]{2,1,0:T(8,128)} %param.19, f32[128,16,128]{2,1,0:T(8,128)S(1)} %gather_fusion.1, pred[128]{0:T(512)(128)(4,1)S(1)} %compare_and_fusion), kind=kOutput, calls=%fused_computation.13 | convolution fusion | flops 403046400 | bytes 9961600 | tf_op jit(solution)/shard_map/kbn,bna->kba/dot_general | solution.py:58
  184.2 0.2 fusion.28
  184.5 0.1 copy_bitcast_fusion.3
  184.5 0.1 broadcast_in_dim.30
  184.7 15.4 %convolution_bitcast_fusion.1 = f32[16,128,128]{2,0,1:T(8,128)S(1)} fusion(f32[16,128,128]{2,0,1:T(8,128)S(1)} %bitcast.122, f32[128,128,128]{2,1,0:T(8,128)} %param.19), kind=kOutput, calls=%fused_computation.5 | convolution fusion | flops 402653184 | bytes 10485760 | tf_op jit(solution)/shard_map/kba,bna->kbn/dot_general | solution.py:72
  200.1 0.8 convolution_bitcast_fusion.5
  200.9 0.7 convolution_bitcast_fusion.3
  201.6 1.6 copy.37
  203.2 0.0 all-gather.5.cloned.1.call-start
  203.3 206.3 %reduce-scatter.3.cloned.1.call-done = f32[16,4,128]{2,0,1:T(8,128)} async-done(((f32[16,128,128]{2,0,1:T(8,128)}), f32[16,4,128]{2,0,1:T(8,128)}) %reduce-scatter.3.cloned.1.call-update) | async-done | bytes 32784 | tf_op jit(solution)/shard_map/reduce_scatter | solution.py:78
  409.6 0.8 slice_add_fusion.1
  410.4 0.2 fusion.27
  410.6 0.6 slice.49
  411.3 20.9 %psum.38 = f32[8192]{0:T(1024)S(1)} all-reduce(f32[8192]{0:T(1024)S(1)} %get-tuple-element.9), channel_id=1, replica_groups=mesh['region'=32,'comm'=8] {'comm'}, use_global_device_ids=true, to_apply=%region_10.13 | all-reduce | flops 8192 | bytes 65536 | tf_op jit(solution)/shard_map/psum | solution.py:67
  432.2 55.1 %all-gather.5.cloned.1.call-done = f32[16,16384]{1,0:T(8,128)} async-done(((f32[16,512]{1,0:T(8,128)}), f32[16,16384]{1,0:T(8,128)}) %all-gather.5.cloned.1.call-update) | async-done | bytes 1048592 | tf_op jit(solution)/shard_map/all_gather | solution.py:52
  487.3 1.3 copy_bitcast_fusion
  488.6 0.6 gather_fusion.2
  489.2 0.1 select_bitcast_fusion
  489.3 0.8 gather_fusion.3
  490.1 9.6 %bitcast_reduce_fusion = f32[16,64,128]{2,0,1:T(8,128)S(1)} fusion(f32[128,128,128]{2,1,0:T(8,128)} %param.19, f32[128,16,128]{2,1,0:T(8,128)S(1)} %gather_fusion.3, pred[128]{0:T(512)(128)(4,1)S(1)} %compare_and_fusion), kind=kOutput, calls=%fused_computation.12 | convolution fusion | flops 403046400 | bytes 9961600 | tf_op jit(solution)/shard_map/kbn,bna->kba/dot_general | solution.py:58
  499.7 0.2 fusion.30
  499.9 0.1 broadcast_in_dim.31
  500.0 15.4 %convolution_bitcast_fusion = f32[16,128,128]{2,0,1:T(8,128)S(1)} fusion(f32[16,128,128]{2,0,1:T(8,128)S(1)} %bitcast.123, f32[128,128,128]{2,1,0:T(8,128)} %param.19), kind=kOutput, calls=%fused_computation.4 | convolution fusion | flops 402653184 | bytes 10485760 | tf_op jit(solution)/shard_map/kba,bna->kbn/dot_general | solution.py:72
  515.4 0.8 convolution_bitcast_fusion.4
  516.2 0.7 convolution_bitcast_fusion.2
  516.9 1.6 copy.44
  518.5 0.1 fusion.31
  518.7 20.7 %psum.39 = f32[8192]{0:T(1024)S(1)} all-reduce(f32[8192]{0:T(1024)S(1)} %fusion.31), channel_id=1, replica_groups=mesh['region'=32,'comm'=8] {'comm'}, use_global_device_ids=true, to_apply=%region_12.15 | all-reduce | flops 8192 | bytes 65536 | tf_op jit(solution)/shard_map/psum | solution.py:67
  539.3 0.6 add_maximum_fusion
  540.0 190.4 %reduce-scatter.5.cloned.1.call-done = f32[16,4,128]{2,0,1:T(8,128)} async-done(((f32[16,128,128]{2,0,1:T(8,128)}), f32[16,4,128]{2,0,1:T(8,128)}) %reduce-scatter.5.cloned.1.call-update) | async-done | bytes 32784 | tf_op jit(solution)/shard_map/reduce_scatter | solution.py:78
  730.3 0.8 slice_add_fusion
  731.1 0.9 fusion.25
  (36 shorter events, 0.5 us)
Async XLA Ops:
  7.2 177.0 %copy-start = (f32[16,8192]{1,0:T(8,128)S(1)}, f32[16,8192]{1,0:T(8,128)}, u32[]{:S(2)}) copy-start(f32[16,8192]{1,0:T(8,128)} %param.13) | copy-start | bytes 1572868
  7.2 177.0 %copy-start.6 = (f32[8192]{0:T(1024)S(1)}, f32[8192]{0:T(1024)}, u32[]{:S(2)}) copy-start(f32[8192]{0:T(1024)} %param.16) | copy-start | bytes 98308
  7.2 177.0 %copy-start.2 = (f32[16,8192]{1,0:T(8,128)S(1)}, f32[16,8192]{1,0:T(8,128)}, u32[]{:S(2)}) copy-start(f32[16,8192]{1,0:T(8,128)} %param.14) | copy-start | bytes 1572868
  7.2 164.6 %all-gather.3.cloned.1.call-start = ((), (), s32[]{:S(2)}) async-start(), calls=%async_computation.2 | async-start | bytes 1081344 | tf_op jit(solution)/shard_map/all_gather | solution.py:52
  8.7 400.9 %reduce-scatter.3.cloned.1.call-start = ((), (), s32[]{:S(2)}) async-start(), calls=%async_computation.3 | async-start | bytes 1081344 | tf_op jit(solution)/shard_map/reduce_scatter | solution.py:78
  184.2 15.9 %copy-start.7 = (s32[128]{0:T(128)S(1)}, s32[128]{0:T(128)}, u32[]{:S(2)}) copy-start(s32[128]{0:T(128)} %param.20) | copy-start | bytes 1540
  184.2 16.6 %copy-start.8 = (s32[8]{0:T(128)S(1)}, s32[8]{0:T(128)}, u32[]{:S(2)}) copy-start(s32[8]{0:T(128)} %param.21) | copy-start | bytes 100
  184.6 225.8 %copy-start.1 = (f32[16,4096]{1,0:T(8,128)S(1)}, f32[16,4096]{1,0:T(8,128)}, u32[]{:S(2)}) copy-start(f32[16,4096]{1,0:T(8,128)} %param.17) | copy-start | bytes 786436
  184.6 225.8 %copy-start.4 = (f32[16,4096]{1,0:T(8,128)S(1)}, f32[16,4096]{1,0:T(8,128)}, u32[]{:S(2)}) copy-start(f32[16,4096]{1,0:T(8,128)} %param.18) | copy-start | bytes 786436
  184.6 247.5 %copy-start.5 = (f32[8192]{0:T(1024)S(1)}, f32[8192]{0:T(1024)}, u32[]{:S(2)}) copy-start(f32[8192]{0:T(1024)} %param.15) | copy-start | bytes 98308
  203.2 284.1 %all-gather.5.cloned.1.call-start = ((), (), s32[]{:S(2)}) async-start(), calls=%async_computation.4 | async-start | bytes 1081344 | tf_op jit(solution)/shard_map/all_gather | solution.py:52
  411.3 319.1 %reduce-scatter.5.cloned.1.call-start = ((), (), s32[]{:S(2)}) async-start(), calls=%async_computation.5 | async-start | bytes 1081344 | tf_op jit(solution)/shard_map/reduce_scatter | solution.py:78
  499.8 18.7 %copy-start.3 = (f32[16,8192]{1,0:T(8,128)}, f32[16,8192]{1,0:T(8,128)S(1)}, u32[]{:S(2)}) copy-start(f32[16,8192]{1,0:T(8,128)S(1)} %get-tuple-element.8) | copy-start | bytes 1572868
Sparse Core Ops, SparseCore 0:
  11.2 78.9 all-gather.2
  203.3 206.2 reduce-scatter.2
  412.8 74.4 all-gather.4
  518.6 211.6 reduce-scatter.4
where the time goes:
time: 739 us
  waiting for transfers between devices  452 us (61%)
  blocking collectives  194 us (26%)
  matrix products  53 us (7%)
  between operations  16.2 us (2%)
  local copies, waits for them, and re-layouts  11.8 us (2%)
  other arithmetic  11.5 us (2%)
    reduce_scatter x2, waiting for transfers between devices, body(): lax.psum_scatter(routed, 'region', scatter_dimension=1, tiled=True)  397 us
    psum x1, blocking collectives, body(): cost_all, demand_all = lax.psum((cost_sq, demand_sq), ('region', 'comm'))  79.2 us
    psum x1, blocking collectives, body(): capacity_all = lax.psum(capacity_sq, 'region')  73.2 us
    all_gather x2, waiting for transfers between devices, body(): lax.all_gather(node_dual[:, :edge_cols], 'region', axis=1, tiled=True)  55.1 us
    psum x2, blocking collectives, body(): load_total = lax.psum(arc_load, 'comm')  41.5 us
    dot_general x2, matrix products, body(): jnp.einsum('kba,bna->kbn', repeated_flow, incidence, precision=highest)  30.9 us
    dot_general x2, matrix products, body(): jnp.einsum('kbn,bna->kba', chosen_duals, incidence, precision=highest)  19.2 us
  transfers between devices with their start and end apart: 4, of which 3 were waited for; matrix products, arithmetic and copies ran while one was open for 1% of the time, Pallas kernels for 0%

commit v1 on v0

--- a/solution.py
+++ b/solution.py
@@ -49,7 +49,12 @@
     flow_now, cap_dual, node_dual = (flow_start, cap_dual_start, node_dual_start)
     edge_cols = NBD * block_width
     for iteration in range(ITERS):
-        bnd_table = lax.all_gather(node_dual[:, :edge_cols], "region", axis=1, tiled=True)
+        bnd_table = jnp.concatenate(
+            lax.all_to_all(
+                jnp.stack([node_dual[:, :edge_cols]] * lax.axis_size("region")), "region", 0, 0
+            ),
+            axis=1,
+        )
         ghost_duals = pick_blocks(bnd_table, ghost_source, commodities, bound_all, block_width)
         dual_blocks = jnp.concatenate(
             [node_dual.reshape(commodities, own_blocks, block_width), ghost_duals], axis=1

time: 739 us -> 712 us (0.963)
  waiting for transfers between devices: 452 us -> 399 us
  starting transfers between devices: 0.16 us -> 18.2 us
    all_gather x2 -> x0, waiting for transfers between devices: 55.1 us -> none  [body(): lax.all_gather(node_dual[:, :edge_cols], 'region', axis=1, tiled=True)]
    all_to_all x0 -> x2, starting transfers between devices: none -> 18.1 us  [body(): lax.all_to_all(jnp.stack([node_dual[:, :edge_cols]] * lax.axis_size('regi...]
where the time goes in v1:
time: 712 us; the launch traced here: 711 us
  waiting for transfers between devices  399 us (56%)
  blocking collectives  195 us (27%)
  matrix products  53.4 us (8%)
  starting transfers between devices  18.2 us (3%)
  between operations  16.5 us (2%)
  other arithmetic  15.1 us (2%)
  local copies, waits for them, and re-layouts  14.1 us (2%)
    reduce_scatter x2, waiting for transfers between devices, body(): lax.psum_scatter(routed, 'region', scatter_dimension=1, tiled=True)  398 us
    psum x1, blocking collectives, body(): cost_all, demand_all = lax.psum((cost_sq, demand_sq), ('region', 'comm'))  77.9 us
    psum x1, blocking collectives, body(): capacity_all = lax.psum(capacity_sq, 'region')  72.6 us
    psum x2, blocking collectives, body(): load_total = lax.psum(arc_load, 'comm')  44.5 us
    dot_general x2, matrix products, body(): jnp.einsum('kba,bna->kbn', repeated_flow, incidence, precision=highest)  31.2 us
    dot_general x2, matrix products, body(): jnp.einsum('kbn,bna->kba', chosen_duals, incidence, precision=highest)  19.3 us
    all_to_all x2, starting transfers between devices, body(): lax.all_to_all(jnp.stack([node_dual[:, :edge_cols]] * lax.axis_size('regi...  18.1 us
  transfers between devices with their start and end apart: 4, of which 3 were waited for; matrix products, arithmetic and copies ran while one was open for 1% of the time, Pallas kernels for 0%

profile of v1, /device:TPU:8, one launch (start us, length us, event | category | flops | bytes accessed | tf_op | source)
XLA Modules:
  0.0 711.2 jit_solution(4864966728687869526)
XLA Ops:
  7.2 0.8 slice.30
  7.9 1.1 stack.4
  9.0 11.3 %all-to-all-start = ((f32[32,16,512]{2,1,0:T(8,128)}), f32[32,16,512]{2,1,0:T(8,128)S(1)}, u32[]{:S(2)}, u32[]{:S(2)}) async-start(f32[32,16,512]{2,1,0:T(8,128)} %stack.4), calls=%async_computation | async-start | bytes 2097152 | tf_op jit(solution)/shard_map/all_to_all | solution.py:53
  20.4 1.6 multiply_reduce_fusion.1
  22.0 1.8 multiply_reduce_fusion
  23.8 1.4 multiply_reduce_fusion.2
  25.2 77.9 %all-reduce = (f32[]{:T(128)}, f32[]{:T(128)}) all-reduce(f32[]{:T(128)} %multiply_reduce_fusion, f32[]{:T(128)} %multiply_reduce_fusion.1), channel_id=1, replica_groups=mesh['region'=32,'comm'=8] {'region','comm'}, use_global_device_ids=true, to_apply=%region_1.0 | all-reduce | flops 2 | bytes 16 | tf_op jit(solution)/shard_map/psum | solution.py:38
  103.1 72.6 %psum.37 = f32[]{:T(128)} all-reduce(f32[]{:T(128)} %multiply_reduce_fusion.2), channel_id=1, replica_groups=mesh['region'=32,'comm'=8] {'region'}, use_global_device_ids=true, to_apply=%region_5.0 | all-reduce | flops 1 | bytes 8 | tf_op jit(solution)/shard_map/psum | solution.py:39
  177.8 0.7 compare_select_fusion.1
  178.4 0.7 compare_select_fusion
  179.1 0.7 compare_and_fusion
  179.8 0.7 compare_and_fusion.1
  180.4 1.7 copy_bitcast_fusion.3
  182.1 0.6 copy.36
  182.8 0.6 copy.37
  183.4 0.6 gather_fusion
  184.1 1.0 pad_maximum_fusion
  185.1 0.8 gather_fusion.1
  185.8 9.6 %bitcast_reduce_fusion.1 = f32[16,64,128]{2,0,1:T(8,128)S(1)} fusion(f32[128,128,128]{2,1,0:T(8,128)} %param.19, f32[128,16,128]{2,1,0:T(8,128)S(1)} %gather_fusion.1, pred[128]{0:T(512)(128)(4,1)S(1)} %compare_and_fusion), kind=kOutput, calls=%fused_computation.11 | convolution fusion | flops 403046400 | bytes 9961600 | tf_op jit(solution)/shard_map/kbn,bna->kba/dot_general | solution.py:63
  195.5 1.3 fusion.28
  197.0 15.6 %convolution_bitcast_fusion.1 = f32[16,128,128]{2,0,1:T(8,128)S(1)} fusion(f32[16,128,128]{2,0,1:T(8,128)S(1)} %bitcast.114, f32[128,128,128]{2,1,0:T(8,128)} %param.19), kind=kOutput, calls=%fused_computation.5 | convolution fusion | flops 402653184 | bytes 10485760 | tf_op jit(solution)/shard_map/kba,bna->kbn/dot_general | solution.py:77
  212.6 0.7 convolution_bitcast_fusion.5
  213.4 0.7 convolution_bitcast_fusion.3
  214.0 1.6 copy.42
  215.7 206.6 %reduce-scatter.3.cloned.1.call-done = f32[16,4,128]{2,0,1:T(8,128)} async-done(((f32[16,128,128]{2,0,1:T(8,128)}), f32[16,4,128]{2,0,1:T(8,128)}) %reduce-scatter.3.cloned.1.call-update) | async-done | bytes 32784 | tf_op jit(solution)/shard_map/reduce_scatter | solution.py:83
  422.3 0.8 slice_add_fusion.1
  423.1 0.2 fusion.27
  423.3 1.1 stack.5
  424.4 6.8 all-to-all-start.1
  431.3 21.0 %psum.38 = f32[8192]{0:T(1024)S(1)} all-reduce(f32[8192]{0:T(1024)S(1)} %get-tuple-element.9), channel_id=1, replica_groups=mesh['region'=32,'comm'=8] {'comm'}, use_global_device_ids=true, to_apply=%region_10.13 | all-reduce | flops 8192 | bytes 65536 | tf_op jit(solution)/shard_map/psum | solution.py:72
  452.3 0.7 copy_bitcast_fusion.2
  453.1 0.8 all-to-all-done.1
  453.8 0.6 copy.44
  454.5 0.6 copy.45
  455.1 0.6 gather_fusion.2
  455.7 0.7 select_bitcast_fusion
  456.4 1.0 pad_maximum_fusion.1
  457.4 0.8 gather_fusion.3
  458.2 9.7 %bitcast_reduce_fusion = f32[16,64,128]{2,0,1:T(8,128)S(1)} fusion(f32[128,128,128]{2,1,0:T(8,128)} %param.19, f32[128,16,128]{2,1,0:T(8,128)S(1)} %gather_fusion.3, pred[128]{0:T(512)(128)(4,1)} %copy-done.13), kind=kOutput, calls=%fused_computation.10 | convolution fusion | flops 403046400 | bytes 9961600 | tf_op jit(solution)/shard_map/kbn,bna->kba/dot_general | solution.py:63
  468.2 15.6 %convolution_bitcast_fusion = f32[16,128,128]{2,0,1:T(8,128)S(1)} fusion(f32[16,128,128]{2,0,1:T(8,128)S(1)} %bitcast.115, f32[128,128,128]{2,1,0:T(8,128)} %param.19), kind=kOutput, calls=%fused_computation.4 | convolution fusion | flops 402653184 | bytes 10485760 | tf_op jit(solution)/shard_map/kba,bna->kbn/dot_general | solution.py:77
  483.8 0.7 convolution_bitcast_fusion.4
  484.6 0.7 convolution_bitcast_fusion.2
  485.3 1.6 copy.50
  487.1 23.5 %psum.39 = f32[8192]{0:T(1024)S(1)} all-reduce(f32[8192]{0:T(1024)S(1)} %fusion.31), channel_id=1, replica_groups=mesh['region'=32,'comm'=8] {'comm'}, use_global_device_ids=true, to_apply=%region_12.15 | all-reduce | flops 8192 | bytes 65536 | tf_op jit(solution)/shard_map/psum | solution.py:72
  510.6 0.6 add_maximum_fusion
  511.2 191.5 %reduce-scatter.5.cloned.1.call-done = f32[16,4,128]{2,0,1:T(8,128)} async-done(((f32[16,128,128]{2,0,1:T(8,128)}), f32[16,4,128]{2,0,1:T(8,128)}) %reduce-scatter.5.cloned.1.call-update) | async-done | bytes 32784 | tf_op jit(solution)/shard_map/reduce_scatter | solution.py:83
  702.6 0.8 slice_add_fusion
  703.5 0.9 fusion.25
  (52 shorter events, 1.1 us)
Async XLA Ops:
  9.0 173.0 %all-to-all-start = ((f32[32,16,512]{2,1,0:T(8,128)}), f32[32,16,512]{2,1,0:T(8,128)S(1)}, u32[]{:S(2)}, u32[]{:S(2)}) async-start(f32[32,16,512]{2,1,0:T(8,128)} %stack.4), calls=%async_computation | async-start | bytes 2097152 | tf_op jit(solution)/shard_map/all_to_all | solution.py:53
  20.4 401.9 %reduce-scatter.3.cloned.1.call-start = ((), (), s32[]{:S(2)}) async-start(), calls=%async_computation.4 | async-start | bytes 1081344 | tf_op jit(solution)/shard_map/reduce_scatter | solution.py:83
  179.8 15.7 %copy-start.13 = (pred[128]{0:T(512)(128)(4,1)}, pred[128]{0:T(512)(128)(4,1)S(1)}, u32[]{:S(2)}) copy-start(pred[128]{0:T(512)(128)(4,1)S(1)} %compare_and_fusion) | copy-start | bytes 388
  180.4 15.0 %copy-start.14 = (pred[8]{0:T(512)(128)(4,1)}, pred[8]{0:T(512)(128)(4,1)S(1)}, u32[]{:S(2)}) copy-start(pred[8]{0:T(512)(128)(4,1)S(1)} %compare_and_fusion.1) | copy-start | bytes 28
  182.7 12.8 %copy-start = (f32[16,8192]{1,0:T(8,128)S(1)}, f32[16,8192]{1,0:T(8,128)}, u32[]{:S(2)}) copy-start(f32[16,8192]{1,0:T(8,128)} %param.13) | copy-start | bytes 1572868
  182.7 12.8 %copy-start.9 = (f32[8192]{0:T(1024)S(1)}, f32[8192]{0:T(1024)}, u32[]{:S(2)}) copy-start(f32[8192]{0:T(1024)} %param.16) | copy-start | bytes 98308
  183.4 13.4 %copy-start.5 = (f32[16,8192]{1,0:T(8,128)S(1)}, f32[16,8192]{1,0:T(8,128)}, u32[]{:S(2)}) copy-start(f32[16,8192]{1,0:T(8,128)} %param.14) | copy-start | bytes 1572868
  195.5 17.1 %copy-start.11 = (s32[128]{0:T(128)S(1)}, s32[128]{0:T(128)}, u32[]{:S(2)}) copy-start(s32[128]{0:T(128)} %param.20) | copy-start | bytes 1540
  195.5 17.8 %copy-start.12 = (s32[8]{0:T(128)S(1)}, s32[8]{0:T(128)}, u32[]{:S(2)}) copy-start(s32[8]{0:T(128)} %param.21) | copy-start | bytes 100
  196.9 226.2 %copy-start.3 = (f32[16,4096]{1,0:T(8,128)S(1)}, f32[16,4096]{1,0:T(8,128)}, u32[]{:S(2)}) copy-start(f32[16,4096]{1,0:T(8,128)} %param.17) | copy-start | bytes 786436
  197.0 226.1 %copy-start.7 = (f32[16,4096]{1,0:T(8,128)S(1)}, f32[16,4096]{1,0:T(8,128)}, u32[]{:S(2)}) copy-start(f32[16,4096]{1,0:T(8,128)} %param.18) | copy-start | bytes 786436
  197.0 255.3 %copy-start.8 = (f32[8192]{0:T(1024)S(1)}, f32[8192]{0:T(1024)}, u32[]{:S(2)}) copy-start(f32[8192]{0:T(1024)} %param.15) | copy-start | bytes 98308
  197.0 255.3 %copy-start.10 = (f32[8192]{0:T(1024)S(1)}, f32[8192]{0:T(1024)}, u32[]{:S(2)}) copy-start(f32[8192]{0:T(1024)} %param.16) | copy-start | bytes 98308
  423.3 32.4 %copy-start.1 = (f32[16,4096]{1,0:T(8,128)}, f32[16,4096]{1,0:T(8,128)S(1)}, u32[]{:S(2)}) copy-start(f32[16,4096]{1,0:T(8,128)S(1)} %fusion.27) | copy-start | bytes 786436
  424.4 29.4 %all-to-all-start.1 = ((f32[32,16,512]{2,1,0:T(8,128)}), f32[32,16,512]{2,1,0:T(8,128)S(1)}, u32[]{:S(2)}, u32[]{:S(2)}) async-start(f32[32,16,512]{2,1,0:T(8,128)} %stack.5), calls=%async_computation.2 | async-start | bytes 2097152 | tf_op jit(solution)/shard_map/all_to_all | solution.py:53
  431.2 271.4 %reduce-scatter.5.cloned.1.call-start = ((), (), s32[]{:S(2)}) async-start(), calls=%async_computation.5 | async-start | bytes 1081344 | tf_op jit(solution)/shard_map/reduce_scatter | solution.py:83
  468.0 18.9 %copy-start.6 = (f32[16,8192]{1,0:T(8,128)}, f32[16,8192]{1,0:T(8,128)S(1)}, u32[]{:S(2)}) copy-start(f32[16,8192]{1,0:T(8,128)S(1)} %get-tuple-element.8) | copy-start | bytes 1572868
  468.2 235.3 %copy-start.2 = (f32[16,4096]{1,0:T(8,128)S(1)}, f32[16,4096]{1,0:T(8,128)}, u32[]{:S(2)}) copy-start(f32[16,4096]{1,0:T(8,128)} %copy-done.1) | copy-start | bytes 786436
  468.2 235.3 %copy-start.4 = (f32[16,4096]{1,0:T(8,128)S(1)}, f32[16,4096]{1,0:T(8,128)}, u32[]{:S(2)}) copy-start(f32[16,4096]{1,0:T(8,128)} %param.17) | copy-start | bytes 786436
Sparse Core Ops, SparseCore 0:
  215.8 206.4 reduce-scatter.2
  487.0 215.5 reduce-scatter.4
